TPU v7x, 512 devices: a whole 4x8x8 slice. The times are simulated.
512 devices in a mesh: region: 16 (over z, core), dev: 32 (over y, x).
Axes of the slice: x: 4, y: 8, z: 8, core: 2. Of those that a mesh axis runs over, the one named last changes fastest.
Arguments:
- basis_values: bfloat16 [6144, 4, 256, 128], P(('region', 'dev')), may hold values from -6 to 6
- density_rows: bfloat16 [1536, 4, 128, 128], P(('region', 'dev')), may hold values from -0.013671875 to 0.013671875
- block_mask: int32 [1536, 4], P(('region', 'dev')), may hold values 0 or 1
- window_start: int32 [512], P(('region', 'dev')), may hold values from 0 to 95
- batch_offsets: int32 [512, 12], P(('region', 'dev')), may hold values from 0 to 28, as said below
- batch_sizes: int32 [512, 12], P(('region', 'dev')), may hold values from 1 to 256, 1920 in all within a row
- atom_near: int32 [6144, 6], P(('region', 'dev')), may hold values from 0 to 1535
- harmonics: bfloat16 [6144, 6, 25, 256], P(('region', 'dev')), may hold values from -6 to 6
- partition: float32 [6144, 6, 256], P(('region', 'dev')), may hold values from 0.002 to 0.05
- radius: float32 [6144, 6, 256], P(('region', 'dev')), may hold values from 0 to 15
- radial_table: float32 [25, 16], replicated, may hold values from -1.5 to 1.5
Outputs:
- density: float32 [6144, 256], P(('region', 'dev'))
- moments: float32 [25, 8192], P(None, ('region', 'dev'))
- potential: float32 [6144, 256], P(('region', 'dev'))
Inputs may be any that keep to these rules, and one draw needn't show every extreme that they name: The blocks of a batch are positions batch_offsets to batch_offsets + 3 of its device's window of 32 consecutive blocks.
All inputs are finite; a program needn't handle non-finite values. No bound on the sum of `block_mask` on one device may be relied on, other than what follows from the above.
Results may differ from a plain program's by a relative error of at most 0.0029.
Values may be sent and summed in bfloat16 or wider, within the bound.
A program may use at most 64 MiB of HBM per device.

v0:
```python
import jax
import jax.numpy as jnp
from jax import lax
from jax.sharding import PartitionSpec as P

ATOM_DEV = 16


def padded_2(cells, sides, width):
    for axis, dim in sides:
        count = lax.axis_size(axis)
        head = lax.slice_in_dim(cells, 0, width, axis=dim)
        tail = lax.slice_in_dim(cells, cells.shape[dim] - width, cells.shape[dim], axis=dim)
        cells = jnp.concatenate(
            [
                lax.ppermute(tail, axis, [(i, (i + 1) % count) for i in range(count)]),
                cells,
                lax.ppermute(head, axis, [((i + 1) % count, i) for i in range(count)]),
            ],
            axis=dim,
        )
    return cells


def spline_basis(radii_row, knot_count):
    knot_points = jnp.arange(knot_count).astype(jnp.float32)
    distance = jnp.abs(radii_row[..., None, :] - knot_points[:, None])
    inner_part = 2.0 / 3.0 - distance * distance + 0.5 * distance * distance * distance
    remote = 2.0 - distance
    outer_part = remote * remote * remote / 6.0
    return jnp.where(distance < 1.0, inner_part, jnp.where(distance < 2.0, outer_part, 0.0))


def batch_density(values, row_blocks):
    block_total = values.shape[0]
    band_width = row_blocks.shape[1]
    leading = jnp.zeros((1,) + values.shape[1:], values.dtype)
    trailing = jnp.zeros((band_width - 2,) + values.shape[1:], values.dtype)
    padded = jnp.concatenate([leading, values, trailing], axis=0)
    stacked = jnp.stack(
        [padded[column : column + block_total] for column in range(band_width)], axis=2
    )
    mixed_rows = jnp.einsum(
        "jpkf,jkgf->jpg", stacked, row_blocks, preferred_element_type=jnp.float32
    )
    return jnp.sum(values.astype(jnp.float32) * mixed_rows, axis=(0, 2))


def per_device(
    basis_values,
    density_rows,
    block_mask,
    window_start,
    batch_offsets,
    batch_sizes,
    atom_near,
    harmonics,
    partition,
    radius,
    radial_table,
):
    dev_count = lax.axis_size("dev")
    blocks_dev = density_rows.shape[0]
    block_count = blocks_dev * dev_count
    masked = density_rows * block_mask.astype(jnp.bfloat16)[:, :, None, None]
    first_block = window_start[0]
    positions = jnp.arange(dev_count, dtype=jnp.int32)
    spatial = (first_block + positions) % block_count
    owner_index = spatial % dev_count
    slot_index = spatial // dev_count
    stored = owner_index * blocks_dev + slot_index
    empty_rows = jnp.zeros((dev_count,) + masked.shape[1:], jnp.bfloat16)
    shard_rows = lax.all_gather(masked, "dev", axis=0, tiled=True)
    inside = (stored >= 0) & (stored < shard_rows.shape[0])
    chosen = jnp.take(shard_rows, jnp.clip(stored, 0, shard_rows.shape[0] - 1), axis=0)
    window = jnp.where(inside[:, None, None, None], chosen, empty_rows)

    def one_density(batch_item):
        values, offset = batch_item
        row_blocks = lax.dynamic_slice_in_dim(window, offset, values.shape[0], 0)
        return batch_density(values, row_blocks)

    point_total = basis_values.shape[2]
    alive_mask = (
        jnp.arange(point_total, dtype=jnp.int32)[None, :] < batch_sizes[0][:, None]
    ).astype(jnp.float32)
    density = lax.map(one_density, (basis_values, batch_offsets[0])) * alive_mask
    moment_terms = jnp.einsum(
        "bip,bilp->bil",
        partition * density[:, None, :],
        harmonics.astype(jnp.float32),
        precision=lax.Precision.HIGHEST,
    )
    comp_total = moment_terms.shape[2]
    atom_region = ATOM_DEV * dev_count
    flattened = atom_near.reshape(-1)
    onehot = (flattened[:, None] == jnp.arange(3 * atom_region, dtype=jnp.int32)[None, :]).astype(
        jnp.float32
    )
    partial_value = jnp.dot(
        moment_terms.reshape(-1, comp_total).T, onehot, precision=lax.Precision.HIGHEST
    )
    partial_value = partial_value.reshape(comp_total, 3, atom_region).transpose(1, 0, 2)
    owner_sums = lax.psum_scatter(partial_value, "dev", scatter_dimension=2, tiled=True)
    side_parts = jnp.stack([owner_sums[0], owner_sums[2]])[None]
    rim_parts = padded_2(side_parts, (("region", 0),), 1)
    moments = owner_sums[1] + rim_parts[0, 1] + rim_parts[2, 0]
    own_table = (moments[:, None, :] * radial_table[:, :, None]).astype(jnp.bfloat16)
    rim_table = padded_2(own_table[None], (("region", 0),), 1)
    spline_table = lax.all_gather(rim_table, "dev", axis=3, tiled=True)
    knot_total = radial_table.shape[1]
    batch_total = atom_near.shape[0]
    near_total = atom_near.shape[1]
    table_flat = spline_table.transpose(1, 2, 0, 3).reshape(comp_total, knot_total, 3 * atom_region)
    selected = jnp.take(table_flat, flattened, axis=2).reshape(
        comp_total, knot_total, batch_total, near_total
    )
    spline = spline_basis(radius, knot_total)
    radial = jnp.einsum(
        "lrbi,birp->bilp", selected.astype(jnp.float32), spline, precision=lax.Precision.HIGHEST
    )
    potential = jnp.sum(harmonics.astype(jnp.float32) * radial, axis=(1, 2)) * alive_mask
    return (density, moments, potential)


def solution(mesh):
    placed = (
        P(("region", "dev"), None, None, None),
        P(("region", "dev"), None, None, None),
        P(("region", "dev"), None),
        P(("region", "dev")),
        P(("region", "dev"), None),
        P(("region", "dev"), None),
        P(("region", "dev"), None),
        P(("region", "dev"), None, None, None),
        P(("region", "dev"), None, None),
        P(("region", "dev"), None, None),
        P(),
    )
    return jax.shard_map(
        per_device,
        mesh=mesh,
        in_specs=placed,
        out_specs=(
            P(("region", "dev"), None),
            P(None, ("region", "dev")),
            P(("region", "dev"), None),
        ),
        check_vma=False,
    )
```

profile of v0, /device:TPU:1, one launch (start us, length us, event | category | flops | bytes accessed | tf_op | source)
XLA Modules:
  0.0 500.1 jit_solution(12459849883825730145)
XLA Ops:
  7.9 1.9 broadcast_multiply_fusion
  10.8 130.3 %all-gather.3.cloned.1.call-done = bf16[96,4,128,128]{3,2,1,0:T(8,128)(2,1)} async-done(((bf16[3,4,128,128]{3,2,1,0:T(8,128)(2,1)}), bf16[96,4,128,128]{3,2,1,0:T(8,128)(2,1)}) %all-gather.3.cloned.1.call-update) | async-done | bytes 12582928 | tf_op jit(solution)/shard_map/all_gather | solution.py:73
  141.0 7.6 %gather_fusion = bf16[32,4,128,128]{3,2,1,0:T(8,128)(2,1)} fusion(bf16[96,4,128,128]{3,2,1,0:T(8,128)(2,1)} %all-gather.3.cloned.1.call-done, s32[1024]{0:T(1024)S(1)} %pad_clamp_fusion.1), kind=kCustom, calls=%fused_computation | custom fusion | bytes 8388736 | tf_op jit(solution)/shard_map/jit(_take)/gather | solution.py:75
  148.6 4.7 select_select_fusion
  153.3 63.6 %while.11 = (s32[]{:T(128)}, f32[12,256]{1,0:T(8,128)S(1)}, bf16[12,4,256,128]{3,2,1,0:T(8,128)(2,1)}, s32[12]{0:T(128)S(1)}, bf16[32,4,128,128]{3,2,1,0:T(8,128)(2,1)}) while((s32[]{:T(128)}, f32[12,256]{1,0:T(8,128)S(1)}, bf16[12,4,256,128]{3,2,1,0:T(8,128)(2,1)}, s32[12]{0:T(128)S(1)}, bf16[32,4,128,128]{3,2,1,0:T(8,128)(2,1)}) %tuple.48), condition=%wide.region_2.3_spmd.clone, body=%wide.region_0.2_spmd.sunk.clone | while | flops 136183552 | bytes 3673207 | solution.py:87
  157.0 1.6 fusion.73
  161.1 1.0 dynamic-slice_bitcast_fusion.4
  162.3 1.6 fusion.73
  167.6 1.6 fusion.73
  172.9 1.6 fusion.73
  178.2 1.6 fusion.73
  183.5 1.6 fusion.73
  188.8 1.6 fusion.73
  194.1 1.6 fusion.73
  199.3 1.6 fusion.73
  204.6 1.6 fusion.73
  209.9 1.6 fusion.73
  215.2 1.6 fusion.73
  217.0 1.0 fusion.41
  218.4 1.4 copy.37
  219.8 1.3 dynamic-slice
  221.7 152.0 %all-reduce.5.cloned.1.call-done = f32[3,25,512]{1,0,2:T(4,128)} async-done(((f32[3,25,512]{1,0,2:T(4,128)}), f32[3,25,512]{1,0,2:T(4,128)}) %all-reduce.5.cloned.1.call-update) | async-done | bytes 153616
  374.7 5.2 %collective-permute-start.1 = (f32[1,2,25,16]{2,1,3,0:T(2,128)S(1)}, f32[1,2,25,16]{2,1,3,0:T(2,128)S(1)}, u32[]{:S(2)}, u32[]{:S(2)}) collective-permute-start(f32[1,2,25,16]{2,1,3,0:T(2,128)S(1)} %maximum_bitcast_fusion), channel_id=1, source_target_pairs={{32,0},{64,32},{96,64},{128,96},{160,128},{192,160},{224,192},{256... | collective-permute-start | bytes 9608 | tf_op jit(solution)/shard_map/ppermute | solution.py:18
  379.9 1.3 collective-permute-start
  381.1 1.4 collective-permute-done.1
  382.6 1.8 collective-permute-start.2
  384.4 1.1 collective-permute-start.3
  386.2 1.9 collective-permute-done.3
  389.1 91.7 %all-gather.5.cloned.1.call-done = bf16[3,25,16,512]{1,2,0,3:T(8,128)(2,1)} async-done(((bf16[3,25,16,16]{1,2,0,3:T(8,128)(2,1)}), bf16[3,25,16,512]{1,2,0,3:T(8,128)(2,1)}) %all-gather.5.cloned.1.call-update) | async-done | bytes 1228816 | tf_op jit(solution)/shard_map/all_gather | solution.py:110
  480.7 6.5 %copy.51 = bf16[25,16,3,512]{0,1,3,2:T(8,128)(2,1)} copy(bf16[25,16,3,512]{0,1,2,3:T(8,128)(2,1)} %bitcast.76) | data formatting | bytes 2457600 | tf_op jit(solution)/shard_map/reshape | solution.py:114
  487.3 3.4 gather_fusion.1
  490.7 2.2 multiply_reduce_fusion
  (101 shorter events, 24.9 us)
Async XLA Ops:
  7.2 3.3 copy-start.3
  7.2 133.9 %all-gather.3.cloned.1.call-start = ((), (), s32[]{:S(2)}) async-start(), calls=%async_computation | async-start | bytes 12976128 | tf_op jit(solution)/shard_map/all_gather | solution.py:73
  9.8 363.9 %all-reduce.5.cloned.1.call-start = ((), (), s32[]{:S(2)}) async-start(), calls=%async_computation.2 | async-start | bytes 2097152
  148.6 4.7 copy-start.8
  153.3 63.6 %copy-start.5 = (s32[1,12]{1,0:T(1,128)S(1)}, s32[1,12]{1,0:T(1,128)}, u32[]{:S(2)}) copy-start(s32[1,12]{1,0:T(1,128)} %param.18) | copy-start | bytes 148
  153.3 63.7 %copy-start = (f32[12,6,256]{2,1,0:T(8,128)S(1)}, f32[12,6,256]{2,1,0:T(8,128)}, u32[]{:S(2)}) copy-start(f32[12,6,256]{2,1,0:T(8,128)} %param.21) | copy-start | bytes 221188
  153.3 63.7 %copy-start.6 = (bf16[12,6,25,256]{3,2,1,0:T(8,128)(2,1)S(1)}, bf16[12,6,25,256]{3,2,1,0:T(8,128)(2,1)}, u32[]{:S(2)}) copy-start(bf16[12,6,25,256]{3,2,1,0:T(8,128)(2,1)} %param.20) | copy-start | bytes 2764804
  216.9 2.8 copy-start.1
  218.4 164.2 %copy-start.4 = (f32[25,16]{0,1:T(8,128)S(1)}, f32[25,16]{0,1:T(8,128)}, u32[]{:S(2)}) copy-start(f32[25,16]{0,1:T(8,128)} %param.23) | copy-start | bytes 4804
  219.8 261.0 %all-gather.5.cloned.1.call-start = ((), (), s32[]{:S(2)}) async-start(), calls=%async_computation.1 | async-start | bytes 6488064 | tf_op jit(solution)/shard_map/all_gather | solution.py:110
  374.7 7.9 %collective-permute-start.1 = (f32[1,2,25,16]{2,1,3,0:T(2,128)S(1)}, f32[1,2,25,16]{2,1,3,0:T(2,128)S(1)}, u32[]{:S(2)}, u32[]{:S(2)}) collective-permute-start(f32[1,2,25,16]{2,1,3,0:T(2,128)S(1)} %maximum_bitcast_fusion), channel_id=1, source_target_pairs={{32,0},{64,32},{96,64},{128,96},{160,128},{192,160},{224,192},{256... | collective-permute-start | bytes 9608 | tf_op jit(solution)/shard_map/ppermute | solution.py:18
  379.9 2.7 collective-permute-start
  382.6 104.7 %copy-start.2 = (f32[25,16]{0,1:T(8,128)}, f32[25,16]{0,1:T(8,128)S(1)}, u32[]{:S(2)}) copy-start(f32[25,16]{0,1:T(8,128)S(1)} %fusion.47) | copy-start | bytes 4804
  382.6 3.5 collective-permute-start.2
  384.4 3.7 collective-permute-start.3
  480.7 10.0 %copy-start.7 = (f32[12,6,256]{2,1,0:T(8,128)S(1)}, f32[12,6,256]{2,1,0:T(8,128)}, u32[]{:S(2)}) copy-start(f32[12,6,256]{2,1,0:T(8,128)} %param.22) | copy-start | bytes 221188
Sparse Core Ops, SparseCore 0:
  11.2 129.8 all-gather.2
  219.9 153.7 all-reduce.4
  389.0 91.7 all-gather.4
where the time goes:
time: 502 us; the launch traced here: 500 us
  waiting for transfers between devices  378 us (75%)
  local copies, waits for them, and re-layouts  43.2 us (9%)
  loops' own time  23.7 us (5%)
  matrix products  22.4 us (4%)
  between operations  15.2 us (3%)
  starting transfers between devices  9.43 us (2%)
  other arithmetic  8.16 us (2%)
    unnamed x4, waiting for transfers between devices  152 us
    all_gather x1, waiting for transfers between devices, per_device(): shard_rows = lax.all_gather(masked, 'dev', axis=0, tiled=True)  130 us
    all_gather x1, waiting for transfers between devices, per_device(): spline_table = lax.all_gather(rim_table, 'dev', axis=3, tiled=True)  91.7 us
    another operation x1, loops' own time, per_device(): lax.map(one_density, (basis_values, batch_offsets[0])) * alive_mask  23.7 us
    dot_general x12, matrix products, batch_density(): jnp.einsum('jpkf,jkgf->jpg', stacked, row_blocks, preferred_element_type=...  18.8 us
    another operation x24, local copies, waits for them, and re-layouts, batch_density(): jnp.stack([padded[column:column + block_total] for column in range(band_w...  13.5 us
  transfers between devices with their start and end apart: 7, of which 6 were waited for; matrix products, arithmetic and copies ran while one was open for 0% of the time, Pallas kernels for 0%

commit v1 on v0

--- a/solution.py
+++ b/solution.py
@@ -70,7 +70,9 @@
     slot_index = spatial // dev_count
     stored = owner_index * blocks_dev + slot_index
     empty_rows = jnp.zeros((dev_count,) + masked.shape[1:], jnp.bfloat16)
-    shard_rows = lax.all_gather(masked, "dev", axis=0, tiled=True)
+    shard_rows = jnp.concatenate(
+        lax.all_to_all(jnp.stack([masked] * lax.axis_size("dev")), "dev", 0, 0), axis=0
+    )
     inside = (stored >= 0) & (stored < shard_rows.shape[0])
     chosen = jnp.take(shard_rows, jnp.clip(stored, 0, shard_rows.shape[0] - 1), axis=0)
     window = jnp.where(inside[:, None, None, None], chosen, empty_rows)

time: 502 us -> 696 us (1.39)
  waiting for transfers between devices: 378 us -> 554 us
  starting transfers between devices: 9.43 us -> 20.1 us
  local copies, waits for them, and re-layouts: 43.2 us -> 50.9 us
    all_to_all x0 -> x1, waiting for transfers between devices: none -> 278 us  [per_device(): lax.all_to_all(jnp.stack([masked] * lax.axis_size('dev')), 'dev', 0, 0)]
    all_gather x1 -> x0, waiting for transfers between devices: 130 us -> none  [per_device(): shard_rows = lax.all_gather(masked, 'dev', axis=0, tiled=True)]
    unnamed x4 -> x3, waiting for transfers between devices: 152 us -> 181 us
    all_to_all x0 -> x1, starting transfers between devices: none -> 10.7 us  [per_device(): lax.all_to_all(jnp.stack([masked] * lax.axis_size('dev')), 'dev', 0, 0)]
    another operation x0 -> x1, local copies, waits for them, and re-layouts: none -> 7.68 us  [per_device(): jnp.stack([masked] * lax.axis_size('dev'))]
where the time goes in v1:
time: 696 us; the launch traced here: 694 us
  waiting for transfers between devices  554 us (80%)
  local copies, waits for them, and re-layouts  50.9 us (7%)
  loops' own time  23.7 us (3%)
  matrix products  22.4 us (3%)
  starting transfers between devices  20.1 us (3%)
  between operations  15.5 us (2%)
  other arithmetic  7.39 us (1%)
    all_to_all x1, waiting for transfers between devices, per_device(): lax.all_to_all(jnp.stack([masked] * lax.axis_size('dev')), 'dev', 0, 0)  278 us
    unnamed x3, waiting for transfers between devices  181 us
    all_gather x1, waiting for transfers between devices, per_device(): spline_table = lax.all_gather(rim_table, 'dev', axis=3, tiled=True)  91.7 us
    another operation x1, loops' own time, per_device(): lax.map(one_density, (basis_values, batch_offsets[0])) * alive_mask  23.7 us
    dot_general x12, matrix products, batch_density(): jnp.einsum('jpkf,jkgf->jpg', stacked, row_blocks, preferred_element_type=...  18.8 us
  transfers between devices with their start and end apart: 7, of which 6 were waited for; matrix products, arithmetic and copies ran while one was open for 0% of the time, Pallas kernels for 0%

profile of v1, /device:TPU:1, one launch (start us, length us, event | category | flops | bytes accessed | tf_op | source)
XLA Modules:
  0.0 694.4 jit_solution(3562708238274735685)
XLA Ops:
  7.8 1.1 broadcast_multiply_fusion
  8.9 7.7 %stack.14 = bf16[32,3,4,128,128]{4,3,2,1,0:T(8,128)(2,1)} broadcast(bf16[3,4,128,128]{3,2,1,0:T(8,128)(2,1)S(1)} %broadcast_multiply_fusion), dimensions={1,2,3,4} | broadcast | bytes 12976128 | tf_op jit(solution)/shard_map/stack | solution.py:74
  16.6 10.7 %all-to-all-start = ((bf16[32,3,4,128,128]{4,3,2,1,0:T(8,128)(2,1)}), bf16[32,3,4,128,128]{4,3,2,1,0:T(8,128)(2,1)}, u32[]{:S(2)}, u32[]{:S(2)}) async-start(bf16[32,3,4,128,128]{4,3,2,1,0:T(8,128)(2,1)} %stack.14), calls=%async_computation | async-start | bytes 25165824 | tf_op jit(solution)/shard_map/all_to_all | solution.py:74
  28.4 278.1 %all-to-all-done = bf16[32,3,4,128,128]{4,3,2,1,0:T(8,128)(2,1)} async-done(((bf16[32,3,4,128,128]{4,3,2,1,0:T(8,128)(2,1)}), bf16[32,3,4,128,128]{4,3,2,1,0:T(8,128)(2,1)}, u32[]{:S(2)}, u32[]{:S(2)}) %all-to-all-start) | async-done | bytes 12582944 | tf_op jit(solution)/shard_map/all_to_all | solution.py:74
  306.4 7.6 %gather_fusion = bf16[32,4,128,128]{3,2,1,0:T(8,128)(2,1)} fusion(bf16[96,4,128,128]{3,2,1,0:T(8,128)(2,1)} %bitcast.13, s32[1024]{0:T(1024)S(1)} %pad_clamp_fusion.1), kind=kCustom, calls=%fused_computation | custom fusion | bytes 8388736 | tf_op jit(solution)/shard_map/jit(_take)/gather | solution.py:77
  314.0 4.7 select_select_fusion
  318.7 63.6 %while.11 = (s32[]{:T(128)}, f32[12,256]{1,0:T(8,128)S(1)}, bf16[12,4,256,128]{3,2,1,0:T(8,128)(2,1)}, s32[12]{0:T(128)S(1)}, bf16[32,4,128,128]{3,2,1,0:T(8,128)(2,1)}) while((s32[]{:T(128)}, f32[12,256]{1,0:T(8,128)S(1)}, bf16[12,4,256,128]{3,2,1,0:T(8,128)(2,1)}, s32[12]{0:T(128)S(1)}, bf16[32,4,128,128]{3,2,1,0:T(8,128)(2,1)}) %tuple.46), condition=%wide.region_2.3_spmd.clone, body=%wide.region_0.2_spmd.sunk.clone | while | flops 136183552 | bytes 3673207 | solution.py:89
  322.4 1.6 fusion.73
  327.7 1.6 fusion.73
  333.0 1.6 fusion.73
  338.3 1.6 fusion.73
  343.6 1.6 fusion.73
  348.9 1.6 fusion.73
  354.2 1.6 fusion.73
  359.5 1.6 fusion.73
  364.8 1.6 fusion.73
  370.1 1.6 fusion.73
  375.4 1.6 fusion.73
  380.7 1.6 fusion.73
  383.8 1.4 copy.37
  385.2 1.3 dynamic-slice
  387.2 180.5 %all-reduce.5.cloned.1.call-done = f32[3,25,512]{1,0,2:T(4,128)} async-done(((f32[3,25,512]{1,0,2:T(4,128)}), f32[3,25,512]{1,0,2:T(4,128)}) %all-reduce.5.cloned.1.call-update) | async-done | bytes 153616
  568.6 5.2 collective-permute-start.1
  573.8 1.3 collective-permute-start
  575.1 1.4 collective-permute-done.1
  576.6 1.8 collective-permute-start.2
  578.3 1.1 collective-permute-start.3
  580.1 1.9 collective-permute-done.3
  583.1 91.7 %all-gather.2.cloned.1.call-done = bf16[3,25,16,512]{1,2,0,3:T(8,128)(2,1)} async-done(((bf16[3,25,16,16]{1,2,0,3:T(8,128)(2,1)}), bf16[3,25,16,512]{1,2,0,3:T(8,128)(2,1)}) %all-gather.2.cloned.1.call-update) | async-done | bytes 1228816 | tf_op jit(solution)/shard_map/all_gather | solution.py:112
  674.7 6.5 copy.51
  681.3 3.4 gather_fusion.1
  684.7 2.2 multiply_reduce_fusion
  (101 shorter events, 26.9 us)
Async XLA Ops:
  16.6 11.5 %copy-start.3 = (s32[12,6]{0,1:T(8,128)S(1)}, s32[12,6]{0,1:T(8,128)}, u32[]{:S(2)}) copy-start(s32[12,6]{0,1:T(8,128)} %param.19) | copy-start | bytes 868
  16.6 289.8 %all-to-all-start = ((bf16[32,3,4,128,128]{4,3,2,1,0:T(8,128)(2,1)}), bf16[32,3,4,128,128]{4,3,2,1,0:T(8,128)(2,1)}, u32[]{:S(2)}, u32[]{:S(2)}) async-start(bf16[32,3,4,128,128]{4,3,2,1,0:T(8,128)(2,1)} %stack.14), calls=%async_computation | async-start | bytes 25165824 | tf_op jit(solution)/shard_map/all_to_all | solution.py:74
  27.4 540.3 %all-reduce.5.cloned.1.call-start = ((), (), s32[]{:S(2)}) async-start(), calls=%async_computation.2 | async-start | bytes 2097152
  314.0 4.7 copy-start.8
  318.7 63.6 %copy-start.5 = (s32[1,12]{1,0:T(1,128)S(1)}, s32[1,12]{1,0:T(1,128)}, u32[]{:S(2)}) copy-start(s32[1,12]{1,0:T(1,128)} %param.18) | copy-start | bytes 148
  318.7 63.7 %copy-start = (f32[12,6,256]{2,1,0:T(8,128)S(1)}, f32[12,6,256]{2,1,0:T(8,128)}, u32[]{:S(2)}) copy-start(f32[12,6,256]{2,1,0:T(8,128)} %param.21) | copy-start | bytes 221188
  318.7 63.7 %copy-start.6 = (bf16[12,6,25,256]{3,2,1,0:T(8,128)(2,1)S(1)}, bf16[12,6,25,256]{3,2,1,0:T(8,128)(2,1)}, u32[]{:S(2)}) copy-start(bf16[12,6,25,256]{3,2,1,0:T(8,128)(2,1)} %param.20) | copy-start | bytes 2764804
  382.4 2.8 copy-start.1
  383.8 192.8 %copy-start.4 = (f32[25,16]{0,1:T(8,128)S(1)}, f32[25,16]{0,1:T(8,128)}, u32[]{:S(2)}) copy-start(f32[25,16]{0,1:T(8,128)} %param.23) | copy-start | bytes 4804
  385.2 289.5 %all-gather.2.cloned.1.call-start = ((), (), s32[]{:S(2)}) async-start(), calls=%async_computation.1 | async-start | bytes 6488064 | tf_op jit(solution)/shard_map/all_gather | solution.py:112
  568.6 7.9 %collective-permute-start.1 = (f32[1,2,25,16]{2,1,3,0:T(2,128)S(1)}, f32[1,2,25,16]{2,1,3,0:T(2,128)S(1)}, u32[]{:S(2)}, u32[]{:S(2)}) collective-permute-start(f32[1,2,25,16]{2,1,3,0:T(2,128)S(1)} %maximum_bitcast_fusion), channel_id=1, source_target_pairs={{32,0},{64,32},{96,64},{128,96},{160,128},{192,160},{224,192},{256... | collective-permute-start | bytes 9608 | tf_op jit(solution)/shard_map/ppermute | solution.py:18
  573.8 2.7 collective-permute-start
  576.6 104.7 %copy-start.2 = (f32[25,16]{0,1:T(8,128)}, f32[25,16]{0,1:T(8,128)S(1)}, u32[]{:S(2)}) copy-start(f32[25,16]{0,1:T(8,128)S(1)} %fusion.47) | copy-start | bytes 4804
  576.6 3.5 collective-permute-start.2
  578.3 3.7 collective-permute-start.3
  674.7 10.0 %copy-start.7 = (f32[12,6,256]{2,1,0:T(8,128)S(1)}, f32[12,6,256]{2,1,0:T(8,128)}, u32[]{:S(2)}) copy-start(f32[12,6,256]{2,1,0:T(8,128)} %param.22) | copy-start | bytes 221188
Sparse Core Ops, SparseCore 0:
  385.3 182.3 all-reduce.4
  583.0 91.7 all-gather.1
